TPU v7x, 32 devices: a whole 2x2x4 slice. The times are simulated.
32 devices in a mesh: pairs: 2 (over y), pb: 4 (over z), ka: 2 (over core), wa: 2 (over x).
Axes of the slice: x: 2, y: 2, z: 4, core: 2. Of those that a mesh axis runs over, the one named last changes fastest.
Arguments:
- clean_rows: bfloat16 [4096, 8192], P(('pairs', 'pb', 'ka'), 'wa'), parts along dimension 0, may hold values from -72 to 72
- noised_rows: bfloat16 [4096, 8192], P(('pairs', 'pb', 'ka'), 'wa'), parts along dimension 0, may hold values from -6 to 6
- query_weight: bfloat16 [8192, 512], P('wa'), may hold values from -0.0625 to 0.0625
- key_weight: bfloat16 [8192, 128], P('wa'), may hold values from -0.0625 to 0.0625
- value_weight: bfloat16 [8192, 128], P('wa'), may hold values from -0.0625 to 0.0625
- out_grads: bfloat16 [4096, 512], P(('pairs', 'pb', 'ka'), 'wa'), parts along dimension 0, may hold values from -6 to 6
- lookback: int32 [4096], P('pairs'), parts along dimension 0, may hold values from 1 to 2048
Outputs:
- attribution: float32 [4096], P(('pairs', 'pb', 'ka', 'wa')), parts along dimension 0
There are 2 independent parts, one for each index of `pairs`. A program takes and returns all parts, laid end to end along the dimension named above; an argument that names none is the same for every part. Nothing has to cross between parts.
All inputs are finite; a program needn't handle non-finite values.
Results may differ from a plain program's by a relative error of at most 0.01315.
The roundings to bfloat16 on the way count: a program that leaves them out, or rounds other values in their place, can miss the bound.
Values may be sent and summed in bfloat16 or wider, within the bound.
No kernel may reach another device: no remote copies, remote signals or barrier semaphores. Data moves between devices by JAX's collectives and lax.ppermute only.
A program may use at most 64 MiB of HBM per device.

v0:
```python
import math

import jax
import jax.numpy as jnp
from jax import lax
from jax.sharding import PartitionSpec as P

very_low = -1e30


def joined(array, axis, combine):
    everything = jax.tree.map(lambda part: lax.all_gather(part, axis), array)
    first = jax.tree.map(lambda part: part[0], everything)

    def turn(k, so_far):
        return combine(so_far, jax.tree.map(lambda part: part[k], everything))

    return lax.fori_loop(1, lax.axis_size(axis), turn, first)


def split_heads(pair_block, head_size):
    return pair_block.reshape(pair_block.shape[0], pair_block.shape[1] // head_size, head_size)


def visible_pairs(query_pos, query_look, key_pos):
    distance = query_pos[:, None] - key_pos[None, :]
    return (distance >= 0) & (distance < query_look[:, None])


def combine_stats(earlier, later):
    highest = jnp.maximum(earlier[0], later[0])
    left_scale = jnp.exp(earlier[0] - highest)
    right_scale = jnp.exp(later[0] - highest)
    return (
        highest,
        earlier[1] * left_scale + later[1] * right_scale,
        earlier[2] * left_scale + later[2] * right_scale,
    )


def block_stats(
    query_block, grad_block, query_pos, query_look, key_block, value_block, key_pos, score_scale
):
    scores = (
        jnp.einsum("bhd,kd->bhk", query_block, key_block, preferred_element_type=jnp.float32)
        * score_scale
    )
    grad_value = jnp.einsum(
        "bhd,kd->bhk", grad_block, value_block, preferred_element_type=jnp.float32
    )
    visible = visible_pairs(query_pos, query_look, key_pos)[:, None, :]
    masked = jnp.where(visible, scores, very_low)
    highest = jnp.max(masked, axis=2)
    weights = jnp.where(visible, jnp.exp(masked - highest[:, :, None]), 0.0)
    return (highest, jnp.sum(weights, axis=2), jnp.sum(weights * grad_value, axis=2))


def block_changes(
    query_block,
    grad_block,
    query_pos,
    query_look,
    row_parts,
    key_block,
    value_block,
    noised_block,
    key_pos,
    score_scale,
):
    highest, row_total, weighted, mean_now = row_parts
    scores = (
        jnp.einsum("bhd,kd->bhk", query_block, key_block, preferred_element_type=jnp.float32)
        * score_scale
    )
    patched = (
        jnp.einsum("bhd,kd->bhk", query_block, noised_block, preferred_element_type=jnp.float32)
        * score_scale
    )
    grad_value = jnp.einsum(
        "bhd,kd->bhk", grad_block, value_block, preferred_element_type=jnp.float32
    )
    visible = visible_pairs(query_pos, query_look, key_pos)[:, None, :]
    held = highest[:, :, None]
    scores = jnp.where(visible, scores, held)
    patched = jnp.where(visible, patched, held)
    shifted = jnp.maximum(held, patched)
    factor = jnp.exp(held - shifted)
    swapped = jnp.exp(patched - shifted) - jnp.exp(scores - shifted)
    divisor = jnp.maximum(row_total[:, :, None] * factor + swapped, 1.0)
    change = (weighted[:, :, None] * factor + swapped * grad_value) / divisor - mean_now[:, :, None]
    return jnp.sum(jnp.where(visible, change, 0.0), axis=(0, 1))


def tile_stats(pair_piece, query_pos, query_look, key_tile, key_pos, score_scale, head_size):
    row_count = pair_piece.shape[0]
    head_cols = pair_piece.shape[1] // 2
    block_rows = math.gcd(row_count, 512)
    key_count = key_tile.shape[0]
    key_width = math.gcd(key_count, 1024)

    def one_block(block_index):
        offset = block_index * block_rows
        pair_block = lax.dynamic_slice_in_dim(pair_piece, offset, block_rows, 0)
        query_block = split_heads(pair_block[:, :head_cols], head_size)
        grad_block = split_heads(pair_block[:, head_cols:], head_size)
        block_pos = lax.dynamic_slice_in_dim(query_pos, offset, block_rows, 0)
        block_look = lax.dynamic_slice_in_dim(query_look, offset, block_rows, 0)
        head_count = query_block.shape[1]

        def one_key(running, key_index):
            key_offset = key_index * key_width
            key_block = lax.dynamic_slice(key_tile, (key_offset, 0), (key_width, head_size))
            value_block = lax.dynamic_slice(
                key_tile, (key_offset, head_size), (key_width, head_size)
            )
            block_keys = lax.dynamic_slice_in_dim(key_pos, key_offset, key_width, 0)
            block_part = block_stats(
                query_block,
                grad_block,
                block_pos,
                block_look,
                key_block,
                value_block,
                block_keys,
                score_scale,
            )
            return (combine_stats(running, block_part), None)

        empty_rows = jnp.zeros((block_rows, head_count), jnp.float32)
        start_stats = (
            jnp.full((block_rows, head_count), very_low, jnp.float32),
            empty_rows,
            empty_rows,
        )
        result, _ = lax.scan(
            one_key, start_stats, jnp.arange(key_count // key_width, dtype=jnp.int32)
        )
        return result

    if block_rows == row_count:
        return one_block(0)
    stacked = lax.map(one_block, jnp.arange(row_count // block_rows, dtype=jnp.int32))
    return tuple((member.reshape(row_count, member.shape[2]) for member in stacked))


def tile_changes(
    pair_tile, query_pos, query_look, merged_stats, key_tile, key_pos, score_scale, head_size
):
    row_count = pair_tile.shape[0]
    head_cols = pair_tile.shape[1] // 2
    block_rows = math.gcd(row_count, 512)
    key_count = key_tile.shape[0]
    key_width = math.gcd(key_count, 1024)
    highest, row_total, weighted = merged_stats
    row_parts = (highest, row_total, weighted, weighted / row_total)

    def one_block(running, block_index):
        offset = block_index * block_rows
        pair_block = lax.dynamic_slice_in_dim(pair_tile, offset, block_rows, 0)
        query_block = split_heads(pair_block[:, :head_cols], head_size)
        grad_block = split_heads(pair_block[:, head_cols:], head_size)
        block_pos = lax.dynamic_slice_in_dim(query_pos, offset, block_rows, 0)
        block_look = lax.dynamic_slice_in_dim(query_look, offset, block_rows, 0)
        block_rows_stats = tuple(
            (lax.dynamic_slice_in_dim(member, offset, block_rows, 0) for member in row_parts)
        )

        def one_key(key_index):
            key_offset = key_index * key_width
            key_block = lax.dynamic_slice(key_tile, (key_offset, 0), (key_width, head_size))
            value_block = lax.dynamic_slice(
                key_tile, (key_offset, head_size), (key_width, head_size)
            )
            noised_block = lax.dynamic_slice(
                key_tile, (key_offset, 2 * head_size), (key_width, head_size)
            )
            block_keys = lax.dynamic_slice_in_dim(key_pos, key_offset, key_width, 0)
            return block_changes(
                query_block,
                grad_block,
                block_pos,
                block_look,
                block_rows_stats,
                key_block,
                value_block,
                noised_block,
                block_keys,
                score_scale,
            )

        changes = lax.map(one_key, jnp.arange(key_count // key_width, dtype=jnp.int32))
        return (running + changes.reshape(key_count), None)

    summed, _ = lax.scan(
        one_block,
        jnp.zeros((key_count,), jnp.float32),
        jnp.arange(row_count // block_rows, dtype=jnp.int32),
    )
    return summed


def shards(clean_rows, noised_rows, query_weight, key_weight, value_weight, out_grads, lookback):
    head_size = key_weight.shape[1]
    score_scale = 1.0 / math.sqrt(head_size)
    pb_size = lax.axis_size("pb")
    ka_size = lax.axis_size("ka")
    pb_index = lax.axis_index("pb")
    ka_index = lax.axis_index("ka")
    pair_rows = clean_rows.shape[0]
    side_weight = jnp.concatenate([key_weight, value_weight], axis=1)
    query_terms = jnp.dot(clean_rows, query_weight, preferred_element_type=jnp.float32)
    queries = lax.psum_scatter(query_terms, "wa", scatter_dimension=1, tiled=True).astype(
        jnp.bfloat16
    )
    key_side = lax.psum_scatter(
        jnp.concatenate(
            [
                jnp.dot(clean_rows, side_weight, preferred_element_type=jnp.float32),
                jnp.dot(noised_rows, key_weight, preferred_element_type=jnp.float32),
            ],
            axis=1,
        ),
        "wa",
        scatter_dimension=0,
        tiled=True,
    ).astype(jnp.bfloat16)
    pair_data = jnp.concatenate([queries, out_grads], axis=1)
    look_grid = lookback.reshape(pb_size, ka_size, pair_rows)
    tile_base = pb_index * (ka_size * pair_rows)
    key_tile = lax.all_gather(key_side, ("pb", "wa"), axis=0, tiled=True)
    row_ids = jnp.arange(key_tile.shape[0], dtype=jnp.int32)
    key_pos = (
        row_ids // pair_rows * (ka_size * pair_rows) + ka_index * pair_rows + row_ids % pair_rows
    )
    look_tile = lax.dynamic_index_in_dim(look_grid, pb_index, 0, keepdims=False).reshape(-1)
    pair_piece = lax.all_gather(pair_data, "ka", axis=0, tiled=True)
    row_ids = jnp.arange(pair_piece.shape[0], dtype=jnp.int32)
    highest, row_total, weighted, pair_tile = tile_stats(
        pair_piece, tile_base + row_ids, look_tile, key_tile, key_pos, score_scale, head_size
    ) + (pair_piece,)
    merged_stats = joined((highest, row_total, weighted), "ka", combine_stats)
    query_pos = tile_base + jnp.arange(pair_tile.shape[0], dtype=jnp.int32)
    key_part = tile_changes(
        pair_tile, query_pos, look_tile, merged_stats, key_tile, key_pos, score_scale, head_size
    )
    return lax.psum_scatter(key_part, ("pb", "wa"), scatter_dimension=0, tiled=True)


def solution(mesh):
    in_specs = (
        P(("pairs", "pb", "ka"), "wa"),
        P(("pairs", "pb", "ka"), "wa"),
        P("wa", None),
        P("wa", None),
        P("wa", None),
        P(("pairs", "pb", "ka"), "wa"),
        P("pairs"),
    )
    out_specs = P(("pairs", "pb", "ka", "wa"))
    return jax.shard_map(shards, mesh=mesh, in_specs=in_specs, out_specs=out_specs, check_vma=False)
```

profile of v0, /device:TPU:0, one launch (start us, length us, event | category | flops | bytes accessed | tf_op | source)
XLA Modules:
  0.0 103.1 jit_solution(1232725400893335930)
XLA Ops:
  6.5 0.0 copy-start
  6.5 0.0 reduce-scatter.5.cloned.1.call-start
  6.5 2.8 %fusion.47 = f32[256,128]{0,1:T(8,128)S(1)} fusion(bf16[256,4096]{1,0:T(8,128)(2,1)} %param.8, bf16[4096,128]{1,0:T(8,128)(2,1)} %param.10), kind=kOutput, calls=%fused_computation.77 | convolution fusion | flops 268435456 | bytes 3276800 | tf_op jit(solution)/shard_map/dot_general | solution.py:219
  9.4 0.0 copy-done
  9.4 2.3 %fusion.10 = f32[256,256]{0,1:T(8,128)S(1)} fusion(bf16[256,4096]{1,0:T(8,128)(2,1)S(1)} %copy-done, bf16[4096,128]{1,0:T(8,128)(2,1)} %param.11, bf16[4096,128]{1,0:T(8,128)(2,1)} %param.10), kind=kOutput, calls=%fused_computation.19 | convolution fusion | flops 541065216 | bytes 4456448 | tf_op jit(solution)/shard_map/dot_general | solution.py:218
  11.7 0.8 pad_maximum_fusion
  12.5 0.0 reduce-scatter.5.cloned.1.call-update
  12.5 0.0 copy-start.2
  12.5 0.0 copy-start.3
  12.5 0.0 copy-start.1
  12.5 0.0 reduce-scatter.3.cloned.1.call-start
  12.6 4.3 %fusion.46 = f32[256,512]{1,0:T(8,128)} fusion(bf16[256,4096]{1,0:T(8,128)(2,1)S(1)} %copy-done, bf16[4096,512]{1,0:T(8,128)(2,1)} %param.9), kind=kOutput, calls=%fused_computation.76 | convolution fusion | flops 1073741824 | bytes 6815744 | tf_op jit(solution)/shard_map/dot_general | solution.py:211
  16.8 0.0 reduce-scatter.3.cloned.1.call-update
  16.9 0.0 copy-done.2
  16.9 0.0 copy-done.3
  17.0 0.6 dynamic-slice
  18.2 0.6 fusion.9
  18.8 9.7 %reduce-scatter.5.cloned.1.call-done = f32[128,384]{0,1:T(8,128)} async-done(((f32[256,384]{0,1:T(8,128)}), f32[128,384]{0,1:T(8,128)}) %reduce-scatter.5.cloned.1.call-update) | async-done | bytes 196624 | tf_op jit(solution)/shard_map/reduce_scatter | solution.py:215
  28.6 0.9 convert_element_type.7
  29.5 32.1 %all_gather.19 = bf16[1024,384]{0,1:T(8,128)(2,1)S(1)} all-gather(bf16[128,384]{0,1:T(8,128)(2,1)S(1)} %convert_element_type.7), channel_id=1, replica_groups=mesh['pairs'=2,'pb'=4,'ka'=2,'wa'=2] {'pb','wa'}, dimensions={0}, use_global_device_ids=true | all-gather | bytes 884736 | tf_op jit(solution)/shard_map/all_gather | solution.py:230
  61.6 0.0 reduce-scatter.3.cloned.1.call-done
  61.6 1.0 convert_element_type.6
  62.6 0.0 copy-done.1
  62.6 2.2 %all_gather.18 = bf16[512,512]{1,0:T(8,128)(2,1)S(1)} all-gather(bf16[256,512]{1,0:T(8,128)(2,1)S(1)} %pad_maximum_fusion.1), channel_id=1, replica_groups=mesh['pairs'=2,'pb'=4,'ka'=2,'wa'=2] {'ka'}, dimensions={0}, use_global_device_ids=true | all-gather | bytes 786432 | tf_op jit(solution)/shard_map/all_gather | solution.py:236
  64.8 1.1 %select_reduce_fusion.1 = (f32[512,2]{0,1:T(2,128)S(1)}, f32[512,2,1024]{2,0,1:T(8,128)S(1)}) fusion(pred[512,1024]{1,0:T(8,128)(4,1)S(1)} %fusion.9, bf16[1024,384]{0,1:T(8,128)(2,1)S(1)} %all_gather.19, bf16[64,2,8,128]{3,2,1,0:T(8,128)(2,1)S(1)} %get-tuple-element.110), kind=kOutput, calls=%fused_computation.10 | convolution fusion | flops 271580160 | bytes 5246976 | tf_op jit(solution)/shard_map/while/body/eval_jaxpr/bhd,kd->bhk/dot_general | solution.py:45
  65.9 2.0 %fusion.4 = (f32[512,2]{0,1:T(2,128)S(1)}, f32[512,2]{0,1:T(2,128)S(1)}, f32[512,2,1024]{2,0,1:T(8,128)S(1)}) fusion(f32[512,2,1024]{2,0,1:T(8,128)S(1)} %get-tuple-element.116, f32[512,2]{0,1:T(2,128)S(1)} %get-tuple-element.115, pred[512,1024]{1,0:T(8,128)(4,1)S(1)} %fusion.9, bf16[1024,384]{0,1:T(8,128)(2,1)S(1)} %all_gather.19, ...), kind=kOutput, calls=%fused_computation.13 | convolution fusion | flops 275773440 | bytes 9449472 | tf_op jit(solution)/shard_map/while/body/eval_jaxpr/bhd,kd->bhk/dot_general | solution.py:48
  67.9 1.8 %all_gather.20 = f32[2,512,2]{1,2,0:T(2,128)S(1)} all-gather(f32[1,512,2]{1,2,0:T(2,128)S(1)} %get-tuple-element.112), channel_id=1, replica_groups=mesh['pairs'=2,'pb'=4,'ka'=2,'wa'=2] {'ka'}, dimensions={0}, use_global_device_ids=true | all-gather | bytes 12288 | tf_op jit(solution)/shard_map/all_gather | solution.py:12
  69.7 1.8 %all_gather.21 = f32[2,512,2]{1,2,0:T(2,128)S(1)} all-gather(f32[1,512,2]{1,2,0:T(2,128)S(1)} %get-tuple-element.114), channel_id=1, replica_groups=mesh['pairs'=2,'pb'=4,'ka'=2,'wa'=2] {'ka'}, dimensions={0}, use_global_device_ids=true | all-gather | bytes 12288 | tf_op jit(solution)/shard_map/all_gather | solution.py:12
  71.5 1.8 %all_gather.22 = f32[2,512,2]{1,2,0:T(2,128)S(1)} all-gather(f32[1,512,2]{1,2,0:T(2,128)S(1)} %get-tuple-element.113), channel_id=1, replica_groups=mesh['pairs'=2,'pb'=4,'ka'=2,'wa'=2] {'ka'}, dimensions={0}, use_global_device_ids=true | all-gather | bytes 12288 | tf_op jit(solution)/shard_map/all_gather | solution.py:12
  73.4 4.5 %select_reduce_fusion = f32[1024]{0:T(1024)S(1)} fusion(f32[512,2,1024]{2,0,1:T(8,128)S(1)} %get-tuple-element.117, f32[512,2,1024]{2,0,1:T(8,128)S(1)} %get-tuple-element.116, f32[512,2]{0,1:T(2,128)S(1)} %get-tuple-element.94, f32[512,2]{0,1:T(2,128)S(1)} %get-tuple-element.107, f32[512,2]{0,1:T(2,128)S(1)} %get-tuple-element.109, ...), kind=kOutput, calls=%fused_computation.7 | convolution fusion | flops 288357376 | bytes 9457664 | tf_op jit(solution)/shard_map/while/body/eval_jaxpr/while/body/eval_jaxpr/bhd,kd->bhk/dot_general | solution.py:76
  77.9 17.8 %all-reduce = f32[1024]{0:T(1024)S(1)} all-reduce(f32[1024]{0:T(1024)S(1)} %select_reduce_fusion), channel_id=4, replica_groups=mesh['pairs'=2,'pb'=4,'ka'=2,'wa'=2] {'pb','wa'}, use_global_device_ids=true, to_apply=%region_6.7.clone | all-reduce | flops 1024 | bytes 8192
  95.7 0.6 dynamic-slice.1
  (9 shorter events, 0.1 us)
Async XLA Ops:
  6.5 2.8 %copy-start = (bf16[256,4096]{1,0:T(8,128)(2,1)S(1)}, bf16[256,4096]{1,0:T(8,128)(2,1)}, u32[]{:S(2)}) copy-start(bf16[256,4096]{1,0:T(8,128)(2,1)} %param.7) | copy-start | bytes 6291460
  6.5 22.0 %reduce-scatter.5.cloned.1.call-start = ((), (), s32[]{:S(2)}) async-start(), calls=%async_computation.3 | async-start | bytes 589824 | tf_op jit(solution)/shard_map/reduce_scatter | solution.py:215
  12.5 4.4 %copy-start.2 = (s32[2048]{0:T(1024)S(1)}, s32[2048]{0:T(1024)}, u32[]{:S(2)}) copy-start(s32[2048]{0:T(1024)} %param.13) | copy-start | bytes 24580
  12.5 4.4 %copy-start.3 = (u32[32]{0:T(128)S(1)}, u32[32]{0:T(128)}, u32[]{:S(2)}) copy-start(u32[32]{0:T(128)} %constant.133) | copy-start | bytes 388
  12.5 50.0 %copy-start.1 = (bf16[256,256]{1,0:T(8,128)(2,1)S(1)}, bf16[256,256]{1,0:T(8,128)(2,1)}, u32[]{:S(2)}) copy-start(bf16[256,256]{1,0:T(8,128)(2,1)} %param.12) | copy-start | bytes 393220
  12.5 49.1 %reduce-scatter.3.cloned.1.call-start = ((), (), s32[]{:S(2)}) async-start(), calls=%async_computation.2 | async-start | bytes 786432 | tf_op jit(solution)/shard_map/reduce_scatter | solution.py:212
Sparse Core Ops, SparseCore 0:
  12.6 15.8 reduce-scatter.4
  30.8 22.4 reduce-scatter.2
where the time goes:
time: 103 us
  blocking collectives  57.5 us (56%)
  matrix products  17 us (17%)
  between operations  14.2 us (14%)
  waiting for transfers between devices  9.76 us (9%)
  other arithmetic  3.36 us (3%)
  local copies, waits for them, and re-layouts  1.25 us (1%)
    all_gather x1, blocking collectives, shards(): key_tile = lax.all_gather(key_side, ('pb', 'wa'), axis=0, tiled=True)  32.1 us
    unnamed x1, blocking collectives  17.8 us
    reduce_scatter x1, waiting for transfers between devices, shards(): lax.psum_scatter(jnp.concatenate([jnp.dot(clean_rows, side_weight, prefer...  9.73 us
    all_gather x3, blocking collectives, joined(): everything = jax.tree.map(lambda part: lax.all_gather(part, axis), array)  5.44 us
    dot_general x1, matrix products, block_changes(): jnp.einsum('bhd,kd->bhk', query_block, noised_block, preferred_element_ty...  4.54 us
    dot_general x1, matrix products, shards(): jnp.dot(clean_rows, query_weight, preferred_element_type=jnp.float32)  4.25 us
    dot_general x1, matrix products, shards(): jnp.dot(noised_rows, key_weight, preferred_element_type=jnp.float32)  2.83 us
    dot_general x1, matrix products, shards(): jnp.dot(clean_rows, side_weight, preferred_element_type=jnp.float32)  2.3 us
  transfers between devices with their start and end apart: 2, of which 1 were waited for; matrix products, arithmetic and copies ran while one was open for 6% of the time, Pallas kernels for 0%

commit v1 on v0

v1 whole, which is shorter than its diff:
```python
import functools
import math

import jax
import jax.numpy as jnp
from jax import lax
from jax.experimental import pallas as pl
from jax.experimental.pallas import tpu as pltpu
from jax.sharding import PartitionSpec as P

very_low = -1e30
plane_axes = ("ka", "wa")


def peer(index, step, size):
    if size & (size - 1) == 0:
        return index ^ step
    return (index + step) % size


def origin(index, step, size):
    if size & (size - 1) == 0:
        return index ^ step
    return (index - step + size) % size


def swapped_with(array, axes, step, size):
    return lax.ppermute(array, axes, [(i, peer(i, step, size)) for i in range(size)])


def pair_step(step_ka, step_wa, ka_size, wa_size):
    moves = []
    for k in range(ka_size):
        for w in range(wa_size):
            target = peer(k, step_ka, ka_size) * wa_size + peer(w, step_wa, wa_size)
            moves.append((k * wa_size + w, target))
    return moves


def dot(a, b):
    return jnp.dot(a, b, preferred_element_type=jnp.float32)


def dot_t(a, b, precision=None):
    return lax.dot_general(
        a, b, (((1,), (1,)), ((), ())), precision=precision, preferred_element_type=jnp.float32
    )


def side_kernel(wa_size, clean_ref, noised_ref, key_ref, value_ref, *rest):
    pieces, total = rest[:-1], rest[-1]
    step = pl.program_id(0)
    head = key_ref.shape[1]
    clean = clean_ref[...]
    both = dot(clean, key_ref[...]), dot(clean, value_ref[...]), dot(noised_ref[...], key_ref[...])

    @pl.when(step == 0)
    def _():
        for n, part in enumerate(both):
            total[:, n * head : (n + 1) * head] = part

    @pl.when(step > 0)
    def _():
        for n, part in enumerate(both):
            total[:, n * head : (n + 1) * head] += part

    @pl.when(step == pl.num_programs(0) - 1)
    def _():
        rows = pieces[0].shape[0]
        mine = lax.axis_index("wa")
        for n, piece in enumerate(pieces):
            start = pl.multiple_of(peer(mine, n, wa_size) * rows, rows)
            piece[...] = total[pl.ds(start, rows), :]


def side_terms(clean_rows, noised_rows, key_weight, value_weight, wa_size):
    rows, depth = clean_rows.shape
    head = key_weight.shape[1]
    chunk = math.gcd(depth, 1024)
    piece = jax.ShapeDtypeStruct((rows // wa_size, 3 * head), jnp.float32)
    wide = pl.BlockSpec((rows, chunk), lambda k: (0, k))
    tall = pl.BlockSpec((chunk, head), lambda k: (k, 0))
    return pl.pallas_call(
        functools.partial(side_kernel, wa_size),
        grid=(depth // chunk,),
        in_specs=[wide, wide, tall, tall],
        out_specs=[pl.BlockSpec(piece.shape, lambda k: (0, 0))] * wa_size,
        out_shape=[piece] * wa_size,
        scratch_shapes=[pltpu.VMEM((rows, 3 * head), jnp.float32)],
        cost_estimate=pl.CostEstimate(
            flops=6 * rows * depth * head,
            bytes_accessed=4 * rows * depth + 4 * depth * head,
            transcendentals=0,
        ),
        name="side_terms",
    )(clean_rows, noised_rows, key_weight, value_weight)


def query_kernel(clean_ref, weight_ref, out_ref):
    step = pl.program_id(0)
    part = dot(clean_ref[...], weight_ref[...])

    @pl.when(step == 0)
    def _():
        out_ref[...] = part

    @pl.when(step > 0)
    def _():
        out_ref[...] += part


def query_terms(clean_rows, query_weight):
    rows, depth = clean_rows.shape
    wide = query_weight.shape[1]
    chunk = math.gcd(depth, 1024)
    return pl.pallas_call(
        query_kernel,
        grid=(depth // chunk,),
        in_specs=[
            pl.BlockSpec((rows, chunk), lambda k: (0, k)),
            pl.BlockSpec((chunk, wide), lambda k: (k, 0)),
        ],
        out_specs=pl.BlockSpec((rows, wide), lambda k: (0, 0)),
        out_shape=jax.ShapeDtypeStruct((rows, wide), jnp.float32),
        cost_estimate=pl.CostEstimate(
            flops=2 * rows * depth * wide,
            bytes_accessed=2 * rows * depth + 2 * depth * wide,
            transcendentals=0,
        ),
        name="query_terms",
    )(clean_rows, query_weight)


class Plan:
    def __init__(self, pb, ka, wa, rows, head, heads):
        self.pb, self.ka, self.wa = pb, ka, wa
        self.rows, self.head, self.heads = rows, head, heads
        self.key_rows = rows // wa
        self.plane = ka * rows
        self.group = heads // wa
        self.factor = math.log2(math.e) / math.sqrt(head)
        self.stats = heads * self.plane


def blocks_of(plan, refs):
    query_refs, grad_refs = refs[: plan.ka], refs[plan.ka : plan.ka + plan.ka * plan.wa]
    ka_index, wa_index = lax.axis_index("ka"), lax.axis_index("wa")
    for a in range(plan.ka):
        first = pl.multiple_of(origin(ka_index, a, plan.ka) * plan.rows, plan.rows)
        for b in range(plan.wa):
            start = origin(wa_index, b, plan.wa) * plan.group
            for k in range(plan.group):
                head = start + k
                lane = pl.multiple_of(head * plan.head, plan.head)
                queries = query_refs[a][:, pl.ds(lane, plan.head)]
                grads = grad_refs[a * plan.wa + b][:, k * plan.head : (k + 1) * plan.head]
                place = pl.multiple_of(head * plan.plane + first, plan.rows)
                yield first, place, queries, grads


def visible_of(plan, step, look_ref, first):
    pb_index = lax.axis_index("pb")
    base = (pb_index - step) * plan.plane
    base += lax.axis_index("ka") * plan.rows + lax.axis_index("wa") * plan.key_rows
    look = look_ref[pl.ds(pb_index, 1), pl.ds(first, plan.rows)]
    query_pos = lax.broadcasted_iota(jnp.int32, (1, plan.rows), 1) + (
        pb_index * plan.plane + first - base
    )
    key_pos = lax.broadcasted_iota(jnp.int32, (plan.key_rows, plan.rows), 0)
    lowest = query_pos - look
    visible = key_pos > lowest
    if step == 0:
        visible &= key_pos <= query_pos
    return visible


def stats_kernel(plan, look_ref, *refs):
    count = plan.ka + plan.ka * plan.wa
    key_refs = refs[count : count + plan.pb]
    out_ref, running = refs[count + plan.pb :]
    pb_index = lax.axis_index("pb")
    size = plan.head

    def one_step(step):
        keys = key_refs[step][:, :size]
        values = key_refs[step][:, size : 2 * size]
        for first, place, queries, grads in blocks_of(plan, refs):
            visible = visible_of(plan, step, look_ref, first)
            scores = dot_t(keys, queries) * plan.factor
            grad_value = dot_t(values, grads)
            scores = jnp.where(visible, scores, very_low).reshape(-1, 8, plan.rows)
            lanes = pl.ds(place, plan.rows)
            highest = jnp.max(scores, axis=0)
            if step > 0:
                earlier = running[0, :, lanes]
                highest = jnp.maximum(earlier, highest)
            weights = jnp.exp2(scores - highest[None])
            total = jnp.sum(weights, axis=0)
            weighted = jnp.sum(weights * grad_value.reshape(weights.shape), axis=0)
            if step > 0:
                scale = jnp.exp2(earlier - highest)
                total += running[1, :, lanes] * scale
                weighted += running[2, :, lanes] * scale
            running[0, :, lanes] = highest
            running[1, :, lanes] = total
            running[2, :, lanes] = weighted

    for step in range(plan.pb):
        if step == 0:
            one_step(step)
        else:
            pl.when(pb_index >= step)(functools.partial(one_step, step))

    highest = running[0]
    top = jnp.max(highest, axis=0, keepdims=True)
    scale = jnp.exp2(highest - top)
    out_ref[:, : plan.stats] = top
    out_ref[:, plan.stats : 2 * plan.stats] = jnp.sum(running[1] * scale, axis=0, keepdims=True)
    out_ref[:, 2 * plan.stats :] = jnp.sum(running[2] * scale, axis=0, keepdims=True)


def changes_kernel(plan, look_ref, *refs):
    count = plan.ka + plan.ka * plan.wa
    key_refs = refs[count : count + plan.pb]
    stats_refs = refs[count + plan.pb : -2]
    out_ref, merged = refs[-2:]
    pb_index = lax.axis_index("pb")
    size = plan.head
    n = plan.stats

    top = functools.reduce(jnp.maximum, [ref[:, :n] for ref in stats_refs])
    scales = [jnp.exp2(ref[:, :n] - top) for ref in stats_refs]
    total = sum(ref[:, n : 2 * n] * scale for ref, scale in zip(stats_refs, scales))
    weighted = sum(ref[:, 2 * n :] * scale for ref, scale in zip(stats_refs, scales))
    merged[0:1, :] = top
    merged[1:2, :] = total
    merged[2:3, :] = weighted
    merged[3:4, :] = weighted / total
    out_ref[...] = jnp.zeros_like(out_ref)

    def one_step(step):
        keys = key_refs[step][:, :size]
        values = key_refs[step][:, size : 2 * size]
        noised = key_refs[step][:, 2 * size :]
        lane_count = min(128, plan.rows)
        summed = jnp.zeros((plan.key_rows, lane_count), jnp.float32)
        for first, place, queries, grads in blocks_of(plan, refs):
            visible = visible_of(plan, step, look_ref, first)
            scores = dot_t(keys, queries) * plan.factor
            patched = dot_t(noised, queries) * plan.factor
            grad_value = dot_t(values, grads)
            lanes = pl.ds(place, plan.rows)
            highest = merged[0:1, lanes]
            row_total = merged[1:2, lanes]
            row_weighted = merged[2:3, lanes]
            mean_now = merged[3:4, lanes]
            shifted = jnp.maximum(highest, patched)
            factor = jnp.exp2(highest - shifted)
            swapped = jnp.exp2(patched - shifted) - jnp.exp2(scores - shifted)
            divisor = jnp.maximum(row_total * factor + swapped, 1.0)
            change = (row_weighted * factor + swapped * grad_value) / divisor - mean_now
            change = jnp.where(visible, change, 0.0)
            for start in range(0, plan.rows, lane_count):
                summed += change[:, start : start + lane_count]
        ones = jnp.ones((8, lane_count), jnp.float32)
        row = dot_t(ones, summed, precision=lax.Precision.HIGHEST)
        out_ref[pl.ds(pb_index - step, 1), :] = row[0:1]

    for step in range(plan.pb):
        if step == 0:
            one_step(step)
        else:
            pl.when(pb_index >= step)(functools.partial(one_step, step))


def whole_block(array):
    return pl.BlockSpec(memory_space=pltpu.VMEM)


def stats_of(plan, look_grid, queries, grads, keys):
    operands = (look_grid, *queries, *grads, *keys)
    return pl.pallas_call(
        functools.partial(stats_kernel, plan),
        in_specs=[whole_block(x) for x in operands],
        out_specs=pl.BlockSpec(memory_space=pltpu.VMEM),
        out_shape=jax.ShapeDtypeStruct((1, 3 * plan.stats), jnp.float32),
        scratch_shapes=[pltpu.VMEM((3, 8, plan.stats), jnp.float32)],
        name="row_stats",
    )(*operands)


def changes_of(plan, look_grid, queries, grads, keys, stats):
    operands = (look_grid, *queries, *grads, *keys, *stats)
    return pl.pallas_call(
        functools.partial(changes_kernel, plan),
        in_specs=[whole_block(x) for x in operands],
        out_specs=pl.BlockSpec(memory_space=pltpu.VMEM),
        out_shape=jax.ShapeDtypeStruct((plan.pb, plan.key_rows), jnp.float32),
        scratch_shapes=[pltpu.VMEM((4, plan.stats), jnp.float32)],
        name="changes",
    )(*operands)


def shards(clean_rows, noised_rows, query_weight, key_weight, value_weight, out_grads, lookback):
    pb_size, ka_size, wa_size = (lax.axis_size(name) for name in ("pb", "ka", "wa"))
    rows = clean_rows.shape[0]
    head = key_weight.shape[1]
    plan = Plan(pb_size, ka_size, wa_size, rows, head, query_weight.shape[1] // head)
    look_grid = lookback.reshape(pb_size, plan.plane)

    pieces = side_terms(clean_rows, noised_rows, key_weight, value_weight, wa_size)
    side = pieces[0]
    for step in range(1, wa_size):
        side = side + swapped_with(pieces[step], "wa", step, wa_size)
    side = side.astype(jnp.bfloat16)

    grads = []
    for a in range(ka_size):
        for b in range(wa_size):
            if a == b == 0:
                grads.append(out_grads)
            else:
                moves = pair_step(a, b, ka_size, wa_size)
                grads.append(lax.ppermute(out_grads, plane_axes, moves))

    terms = query_terms(clean_rows, query_weight)
    summed = terms
    for step in range(1, wa_size):
        summed = summed + swapped_with(terms, "wa", step, wa_size)
    own = summed.astype(jnp.bfloat16)
    queries = [own]
    for step in range(1, ka_size):
        queries.append(swapped_with(own, "ka", step, ka_size))

    keys = [side]
    for step in range(1, pb_size):
        keys.append(lax.ppermute(side, "pb", [(i, i + step) for i in range(pb_size - step)]))

    mine = stats_of(plan, look_grid, queries, grads, keys)
    stats = [mine]
    for a in range(ka_size):
        for b in range(wa_size):
            if a or b:
                moves = pair_step(a, b, ka_size, wa_size)
                stats.append(lax.ppermute(mine, plane_axes, moves))
    part = changes_of(plan, look_grid, queries, grads, keys, stats)
    gathered = lax.all_to_all(part, "pb", 0, 0, tiled=True)
    return jnp.sum(gathered, axis=0)


def solution(mesh):
    in_specs = (
        P(("pairs", "pb", "ka"), "wa"),
        P(("pairs", "pb", "ka"), "wa"),
        P("wa", None),
        P("wa", None),
        P("wa", None),
        P(("pairs", "pb", "ka"), "wa"),
        P("pairs"),
    )
    out_specs = P(("pairs", "pb", "ka", "wa"))
    return jax.shard_map(shards, mesh=mesh, in_specs=in_specs, out_specs=out_specs, check_vma=False)
```

time: 103 us -> 73.9 us (0.72)
  blocking collectives: 57.5 us -> 17.3 us
  matrix products: 17 us -> 0 us
  starting transfers between devices: 0.04 us -> 16.9 us
  Pallas kernels: 0 us -> 16.6 us
  between operations: 14.2 us -> 0.17 us
  waiting for transfers between devices: 9.76 us -> 18.6 us
  other arithmetic: 3.36 us -> 1.57 us
  local copies, waits for them, and re-layouts: 1.25 us -> 2.53 us
    all_gather x5 -> x0, blocking collectives: 39.7 us -> none  [the longest x1 32.1 us: shards(): key_tile = lax.all_gather(key_side, ('pb', 'wa'), axis=0, tiled=True)]
    ppermute x0 -> x12, waiting for transfers between devices: none -> 18.6 us  [the longest x3 14.2 us: swapped_with(): lax.ppermute(array, axes, [(i, peer(i, step, size)) for i in range(size)])]
    unnamed x1 -> x0, blocking collectives: 17.8 us -> none
    all_to_all x0 -> x1, blocking collectives: none -> 17.3 us  [shards(): gathered = lax.all_to_all(part, 'pb', 0, 0, tiled=True)]
    dot_general x6 -> x0, matrix products: 17 us -> none  [the longest x1 4.54 us: block_changes(): jnp.einsum('bhd,kd->bhk', query_block, noised_block, preferred_element_ty...]
    ppermute x0 -> x12, starting transfers between devices: none -> 16.9 us  [the longest x3 9.46 us: shards(): lax.ppermute(side, 'pb', [(i, i + step) for i in range(pb_size - step)])]
    pallas_call x0 -> x4, Pallas kernels: none -> 16.6 us  [the longest x1 5.43 us: side_terms(): pl.pallas_call(functools.partial(side_kernel, wa_size), grid=(depth // ch...]
    reduce_scatter x2 -> x0, waiting for transfers between devices: 9.73 us -> none  [the longest x1 9.73 us: shards(): lax.psum_scatter(jnp.concatenate([jnp.dot(clean_rows, side_weight, prefer...]
  transfers between devices with their start and end apart: 2 -> 12, of which waited for: 1 -> 6; matrix products, arithmetic and copies ran while one was open for 6% -> 2% of each run, Pallas kernels for 0% -> 7%
where the time goes in v1:
time: 73.9 us; the launch traced here: 73.5 us
  waiting for transfers between devices  18.6 us (25%)
  blocking collectives  17.3 us (23%)
  starting transfers between devices  16.9 us (23%)
  Pallas kernels  16.6 us (22%)
  local copies, waits for them, and re-layouts  2.53 us (3%)
  other arithmetic  1.57 us (2%)
    all_to_all x1, blocking collectives, shards(): gathered = lax.all_to_all(part, 'pb', 0, 0, tiled=True)  17.3 us
    ppermute x3, waiting for transfers between devices, swapped_with(): lax.ppermute(array, axes, [(i, peer(i, step, size)) for i in range(size)])  14.2 us
    ppermute x3, starting transfers between devices, shards(): lax.ppermute(side, 'pb', [(i, i + step) for i in range(pb_size - step)])  9.46 us
    pallas_call x1, Pallas kernels, side_terms(): pl.pallas_call(functools.partial(side_kernel, wa_size), grid=(depth // ch...  5.43 us
    pallas_call x1, Pallas kernels, query_terms(): pl.pallas_call(query_kernel, grid=(depth // chunk,), in_specs=[pl.BlockSp...  5.17 us
    pallas_call x1, Pallas kernels, changes_of(): pl.pallas_call(functools.partial(changes_kernel, plan), in_specs=[whole_b...  3.33 us
    ppermute x3, starting transfers between devices, swapped_with(): lax.ppermute(array, axes, [(i, peer(i, step, size)) for i in range(size)])  3.12 us
    ppermute x3, waiting for transfers between devices, shards(): stats.append(lax.ppermute(mine, plane_axes, moves))  2.81 us
  transfers between devices with their start and end apart: 12, of which 6 were waited for; matrix products, arithmetic and copies ran while one was open for 2% of the time, Pallas kernels for 7%

profile of v1, /device:TPU:0, one launch (start us, length us, event | category | flops | bytes accessed | tf_op | source)
XLA Modules:
  0.0 73.5 jit_solution(9246081203880972394)
XLA Ops:
  0.0 0.0 copy-start.4
  0.0 5.2 %query_terms.1 = f32[256,512]{1,0:T(8,128)} custom-call(bf16[256,4096]{1,0:T(8,128)(2,1)} %clean_ref.3, bf16[4096,512]{1,0:T(8,128)(2,1)} %weight_ref.1), custom_call_target="tpu_custom_call" | custom-call | flops 1073741824 | bytes 6291456 | tf_op jit(solution)/shard_map/query_terms/pallas_call | solution.py:116
  5.2 0.0 copy-start.1
  5.2 0.0 copy-start.14
  5.2 3.0 %collective-permute-start = (f32[256,512]{1,0:T(8,128)}, f32[256,512]{1,0:T(8,128)S(1)}, u32[]{:S(2)}, u32[]{:S(2)}) collective-permute-start(f32[256,512]{1,0:T(8,128)} %query_terms.1), channel_id=1, source_target_pairs={{0,1},{1,0},{2,3},{3,2},{4,5},{5,4},{6,7},{7,6},{8,9},{9,8},{10,11... | collective-permute-start | bytes 1572872 | tf_op jit(solution)/shard_map/ppermute | solution.py:28
  8.2 0.0 copy-done.4
  8.2 0.1 collective-permute-start.2
  8.2 0.0 collective-permute-start.3
  8.2 2.1 %collective-permute-start.4 = (bf16[256,256]{1,0:T(8,128)(2,1)S(1)}, bf16[256,256]{1,0:T(8,128)(2,1)S(1)}, u32[]{:S(2)}, u32[]{:S(2)}) collective-permute-start(bf16[256,256]{1,0:T(8,128)(2,1)S(1)} %copy-done.4), channel_id=1, source_target_pairs={{0,3},{1,2},{2,1},{3,0},{4,7},{5,6},{6,5},{7,4},{8,11},{9,10},{10,... | collective-permute-start | bytes 393224 | tf_op jit(solution)/shard_map/ppermute | solution.py:324
  10.3 5.4 %side_terms.1 = (f32[128,384]{1,0:T(8,128)}, f32[128,384]{1,0:T(8,128)}) custom-call(bf16[256,4096]{1,0:T(8,128)(2,1)} %clean_ref.3, bf16[256,4096]{1,0:T(8,128)(2,1)} %noised_ref.1, bf16[4096,128]{1,0:T(8,128)(2,1)} %key_ref.1, bf16[4096,128]{1,0:T(8,128)(2,1)} %value_ref.1), custom_call_target="tpu_custom_call" | custom-call | flops 805306368 | bytes 6291456 | tf_op jit(solution)/shard_map/side_terms/pallas_call | solution.py:83
  15.7 0.1 collective-permute-start.5
  15.8 5.4 %collective-permute-done = f32[256,512]{1,0:T(8,128)S(1)} collective-permute-done((f32[256,512]{1,0:T(8,128)}, f32[256,512]{1,0:T(8,128)S(1)}, u32[]{:S(2)}, u32[]{:S(2)}) %collective-permute-start) | collective-permute-done | bytes 524320 | tf_op jit(solution)/shard_map/ppermute | solution.py:28
  21.2 0.0 copy-done.1
  21.2 0.1 add_convert_fusion.refs_0_
  21.3 0.0 copy-start
  21.3 0.1 collective-permute-start.1
  21.4 8.8 %collective-permute-done.5 = f32[128,384]{1,0:T(8,128)S(1)} collective-permute-done((f32[128,384]{1,0:T(8,128)}, f32[128,384]{1,0:T(8,128)S(1)}, u32[]{:S(2)}, u32[]{:S(2)}) %collective-permute-start.5) | collective-permute-done | bytes 196640 | tf_op jit(solution)/shard_map/ppermute | solution.py:28
  30.2 1.0 %add_convert_fusion.1.refs_6_ = bf16[128,384]{1,0:T(8,128)(2,1)S(1)} fusion(f32[128,384]{1,0:T(8,128)} %get-tuple-element.7, f32[128,384]{1,0:T(8,128)S(1)} %collective-permute-done.5), kind=kLoop, calls=%fused_computation.1 | loop fusion | flops 98304 | bytes 491520 | tf_op jit(solution)/shard_map/convert_element_type | solution.py:315
  31.1 0.0 copy-start.3
  31.1 3.7 %collective-permute-start.6 = (bf16[128,384]{1,0:T(8,128)(2,1)S(1)}, bf16[128,384]{1,0:T(8,128)(2,1)S(1)}, u32[]{:S(2)}, u32[]{:S(2)}) collective-permute-start(bf16[128,384]{1,0:T(8,128)(2,1)S(1)} %add_convert_fusion.1.refs_6_), channel_id=1, source_target_pairs={{0,4},{4,8},{8,12},{1,5},{5,9},{9,13},{2,6},{6,10},{10,14},{3,7},{... | collective-permute-start | bytes 294920 | tf_op jit(solution)/shard_map/ppermute | solution.py:337
  34.8 0.0 collective-permute-done.2.refs_3_
  34.8 0.0 copy-start.5
  34.8 4.5 %collective-permute-start.7 = (bf16[128,384]{1,0:T(8,128)(2,1)S(1)}, bf16[128,384]{1,0:T(8,128)(2,1)S(1)}, u32[]{:S(2)}, u32[]{:S(2)}) collective-permute-start(bf16[128,384]{1,0:T(8,128)(2,1)S(1)} %add_convert_fusion.1.refs_6_), channel_id=1, source_target_pairs={{0,8},{4,12},{1,9},{5,13},{2,10},{6,14},{3,11},{7,15},{16,24},{20,... | collective-permute-start | bytes 294920 | tf_op jit(solution)/shard_map/ppermute | solution.py:337
  39.3 0.0 collective-permute-done.3.refs_4_
  39.4 0.0 copy-start.6
  39.4 1.3 %collective-permute-start.8 = (bf16[128,384]{1,0:T(8,128)(2,1)S(1)}, bf16[128,384]{1,0:T(8,128)(2,1)S(1)}, u32[]{:S(2)}, u32[]{:S(2)}) collective-permute-start(bf16[128,384]{1,0:T(8,128)(2,1)S(1)} %add_convert_fusion.1.refs_6_), channel_id=1, source_target_pairs={{0,12},{1,13},{2,14},{3,15},{16,28},{17,29},{18,30},{19,31}} | collective-permute-start | bytes 294920 | tf_op jit(solution)/shard_map/ppermute | solution.py:337
  40.7 0.0 copy-done.14
  40.7 0.6 reshape.5.look_ref
  41.3 0.0 collective-permute-done.4.refs_5_
  41.3 0.0 copy-start.7
  41.3 0.0 collective-permute-done.6.refs_7_
  41.3 0.0 copy-start.8
  41.3 0.3 collective-permute-done.7.refs_8_
  41.6 0.0 copy-start.9
  41.6 1.3 %collective-permute-done.8.refs_9_ = bf16[128,384]{1,0:T(8,128)(2,1)S(1)} collective-permute-done((bf16[128,384]{1,0:T(8,128)(2,1)S(1)}, bf16[128,384]{1,0:T(8,128)(2,1)S(1)}, u32[]{:S(2)}, u32[]{:S(2)}) %collective-permute-start.8) | collective-permute-done | bytes 98336 | tf_op jit(solution)/shard_map/ppermute | solution.py:337
  42.9 0.0 copy-start.10
  42.9 0.0 collective-permute-done.1.refs_1_
  42.9 0.0 copy-done
  42.9 0.0 copy-done.3
  42.9 0.0 copy-done.5
  42.9 0.0 copy-done.6
  42.9 0.0 copy-done.7
  42.9 0.0 copy-done.8
  42.9 0.0 copy-done.9
  42.9 0.6 copy-done.10
  43.5 0.0 copy-start.2
  43.5 0.7 copy-done.2
  44.2 2.7 %row_stats.1.refs_10_ = f32[1,6144]{1,0:T(1,128)} custom-call(s32[4,512]{1,0:T(4,128)} %reshape.5.look_ref, bf16[256,512]{1,0:T(8,128)(2,1)} %copy-done, bf16[256,512]{1,0:T(8,128)(2,1)} %copy-done.2, bf16[256,256]{1,0:T(8,128)(2,1)} %refs_2_.3, bf16[256,256]{1,0:T(8,128)(2,1)} %copy-done.5, bf16[256,256]{1,0:T(8,128)(2,1)} %copy-done.6, ...), custom_call_target="tpu_custom_call" | custom-call | tf_op jit(solution)/shard_map/row_stats/pallas_call | solution.py:282
  46.9 1.5 %collective-permute-start.9 = (f32[1,6144]{1,0:T(1,128)}, f32[1,6144]{1,0:T(1,128)S(1)}, u32[]{:S(2)}, u32[]{:S(2)}) collective-permute-start(f32[1,6144]{1,0:T(1,128)} %row_stats.1.refs_10_), channel_id=1, source_target_pairs={{0,1},{1,0},{2,3},{3,2},{4,5},{5,4},{6,7},{7,6},{8,9},{9,8},{10,11... | collective-permute-start | bytes 73736 | tf_op jit(solution)/shard_map/ppermute | solution.py:345
  48.4 0.0 collective-permute-start.10
  48.4 0.7 collective-permute-start.11
  49.0 1.9 %collective-permute-done.9.refs_11_ = f32[1,6144]{1,0:T(1,128)S(1)} collective-permute-done((f32[1,6144]{1,0:T(1,128)}, f32[1,6144]{1,0:T(1,128)S(1)}, u32[]{:S(2)}, u32[]{:S(2)}) %collective-permute-start.9) | collective-permute-done | bytes 24608 | tf_op jit(solution)/shard_map/ppermute | solution.py:345
  50.9 0.0 copy-start.11
  50.9 0.0 collective-permute-done.10.refs_12_
  50.9 0.0 copy-start.12
  50.9 0.9 %collective-permute-done.11.refs_13_ = f32[1,6144]{1,0:T(1,128)S(1)} collective-permute-done((f32[1,6144]{1,0:T(1,128)}, f32[1,6144]{1,0:T(1,128)S(1)}, u32[]{:S(2)}, u32[]{:S(2)}) %collective-permute-start.11) | collective-permute-done | bytes 24608 | tf_op jit(solution)/shard_map/ppermute | solution.py:345
  51.8 0.0 copy-done.11
  51.8 0.0 copy-done.12
  51.8 0.0 copy-start.13
  51.8 0.6 copy-done.13
  52.4 3.3 %changes.1 = f32[4,128]{1,0:T(4,128)} custom-call(s32[4,512]{1,0:T(4,128)} %reshape.5.look_ref, bf16[256,512]{1,0:T(8,128)(2,1)} %copy-done, bf16[256,512]{1,0:T(8,128)(2,1)} %copy-done.2, bf16[256,256]{1,0:T(8,128)(2,1)} %refs_2_.3, bf16[256,256]{1,0:T(8,128)(2,1)} %copy-done.5, bf16[256,256]{1,0:T(8,128)(2,1)} %copy-done.6, bf16[256,256]{1,0:T(8,128)(2,1)} %copy-done.7, ...), custom_call_target="tpu_custom_call" | custom-call | tf_op jit(solution)/shard_map/changes/pallas_call | solution.py:294
  55.8 17.3 %all_to_all.9 = f32[4,1,128]{2,1,0:T(1,128)S(1)} all-to-all(f32[4,1,128]{2,1,0:T(1,128)} %bitcast.3), channel_id=1, replica_groups=mesh['pairs'=2,'pb'=4,'ka'=2,'wa'=2] {'pb'}, dimensions={0} | all-to-all | bytes 4096 | tf_op jit(solution)/shard_map/all_to_all | solution.py:347
  73.0 0.5 reduce_sum.9
Async XLA Ops:
  0.0 8.2 %copy-start.4 = (bf16[256,256]{1,0:T(8,128)(2,1)S(1)}, bf16[256,256]{1,0:T(8,128)(2,1)}, u32[]{:S(2)}) copy-start(bf16[256,256]{1,0:T(8,128)(2,1)} %refs_2_.3) | copy-start | bytes 393220
  5.2 16.0 %copy-start.1 = (f32[256,512]{1,0:T(8,128)S(1)}, f32[256,512]{1,0:T(8,128)}, u32[]{:S(2)}) copy-start(f32[256,512]{1,0:T(8,128)} %query_terms.1) | copy-start | bytes 1572868
  5.2 35.5 %copy-start.14 = (s32[2048]{0:T(1024)S(1)}, s32[2048]{0:T(1024)}, u32[]{:S(2)}) copy-start(s32[2048]{0:T(1024)} %param.13) | copy-start | bytes 24580
  5.2 16.0 %collective-permute-start = (f32[256,512]{1,0:T(8,128)}, f32[256,512]{1,0:T(8,128)S(1)}, u32[]{:S(2)}, u32[]{:S(2)}) collective-permute-start(f32[256,512]{1,0:T(8,128)} %query_terms.1), channel_id=1, source_target_pairs={{0,1},{1,0},{2,3},{3,2},{4,5},{5,4},{6,7},{7,6},{8,9},{9,8},{10,11... | collective-permute-start | bytes 1572872 | tf_op jit(solution)/shard_map/ppermute | solution.py:28
  8.2 26.7 %collective-permute-start.2 = (bf16[256,256]{1,0:T(8,128)(2,1)S(1)}, bf16[256,256]{1,0:T(8,128)(2,1)S(1)}, u32[]{:S(2)}, u32[]{:S(2)}) collective-permute-start(bf16[256,256]{1,0:T(8,128)(2,1)S(1)} %copy-done.4), channel_id=1, source_target_pairs={{0,1},{1,0},{2,3},{3,2},{4,5},{5,4},{6,7},{7,6},{8,9},{9,8},{10,11... | collective-permute-start | bytes 393224 | tf_op jit(solution)/shard_map/ppermute | solution.py:324
  8.2 31.1 %collective-permute-start.3 = (bf16[256,256]{1,0:T(8,128)(2,1)S(1)}, bf16[256,256]{1,0:T(8,128)(2,1)S(1)}, u32[]{:S(2)}, u32[]{:S(2)}) collective-permute-start(bf16[256,256]{1,0:T(8,128)(2,1)S(1)} %copy-done.4), channel_id=1, source_target_pairs={{0,2},{1,3},{2,0},{3,1},{4,6},{5,7},{6,4},{7,5},{8,10},{9,11},{10,... | collective-permute-start | bytes 393224 | tf_op jit(solution)/shard_map/ppermute | solution.py:324
  8.2 33.0 %collective-permute-start.4 = (bf16[256,256]{1,0:T(8,128)(2,1)S(1)}, bf16[256,256]{1,0:T(8,128)(2,1)S(1)}, u32[]{:S(2)}, u32[]{:S(2)}) collective-permute-start(bf16[256,256]{1,0:T(8,128)(2,1)S(1)} %copy-done.4), channel_id=1, source_target_pairs={{0,3},{1,2},{2,1},{3,0},{4,7},{5,6},{6,5},{7,4},{8,11},{9,10},{10,... | collective-permute-start | bytes 393224 | tf_op jit(solution)/shard_map/ppermute | solution.py:324
  15.7 14.5 %collective-permute-start.5 = (f32[128,384]{1,0:T(8,128)}, f32[128,384]{1,0:T(8,128)S(1)}, u32[]{:S(2)}, u32[]{:S(2)}) collective-permute-start(f32[128,384]{1,0:T(8,128)} %get-tuple-element.8), channel_id=1, source_target_pairs={{0,1},{1,0},{2,3},{3,2},{4,5},{5,4},{6,7},{7,6},{8,9},{9,8},{10,11... | collective-permute-start | bytes 589832 | tf_op jit(solution)/shard_map/ppermute | solution.py:28
  21.3 21.6 %copy-start = (bf16[256,512]{1,0:T(8,128)(2,1)}, bf16[256,512]{1,0:T(8,128)(2,1)S(1)}, u32[]{:S(2)}) copy-start(bf16[256,512]{1,0:T(8,128)(2,1)S(1)} %add_convert_fusion.refs_0_) | copy-start | bytes 786436
  21.3 21.6 %collective-permute-start.1 = (bf16[256,512]{1,0:T(8,128)(2,1)S(1)}, bf16[256,512]{1,0:T(8,128)(2,1)S(1)}, u32[]{:S(2)}, u32[]{:S(2)}) collective-permute-start(bf16[256,512]{1,0:T(8,128)(2,1)S(1)} %add_convert_fusion.refs_0_), channel_id=1, source_target_pairs={{0,2},{2,0},{1,3},{3,1},{4,6},{6,4},{5,7},{7,5},{8,10},{10,8},{9,1... | collective-permute-start | bytes 786440 | tf_op jit(solution)/shard_map/ppermute | solution.py:28
  31.1 11.7 %copy-start.3 = (bf16[128,384]{1,0:T(8,128)(2,1)}, bf16[128,384]{1,0:T(8,128)(2,1)S(1)}, u32[]{:S(2)}) copy-start(bf16[128,384]{1,0:T(8,128)(2,1)S(1)} %add_convert_fusion.1.refs_6_) | copy-start | bytes 294916
  31.1 10.1 %collective-permute-start.6 = (bf16[128,384]{1,0:T(8,128)(2,1)S(1)}, bf16[128,384]{1,0:T(8,128)(2,1)S(1)}, u32[]{:S(2)}, u32[]{:S(2)}) collective-permute-start(bf16[128,384]{1,0:T(8,128)(2,1)S(1)} %add_convert_fusion.1.refs_6_), channel_id=1, source_target_pairs={{0,4},{4,8},{8,12},{1,5},{5,9},{9,13},{2,6},{6,10},{10,14},{3,7},{... | collective-permute-start | bytes 294920 | tf_op jit(solution)/shard_map/ppermute | solution.py:337
  34.8 8.0 %copy-start.5 = (bf16[256,256]{1,0:T(8,128)(2,1)}, bf16[256,256]{1,0:T(8,128)(2,1)S(1)}, u32[]{:S(2)}) copy-start(bf16[256,256]{1,0:T(8,128)(2,1)S(1)} %collective-permute-done.2.refs_3_) | copy-start | bytes 393220
  34.8 6.7 %collective-permute-start.7 = (bf16[128,384]{1,0:T(8,128)(2,1)S(1)}, bf16[128,384]{1,0:T(8,128)(2,1)S(1)}, u32[]{:S(2)}, u32[]{:S(2)}) collective-permute-start(bf16[128,384]{1,0:T(8,128)(2,1)S(1)} %add_convert_fusion.1.refs_6_), channel_id=1, source_target_pairs={{0,8},{4,12},{1,9},{5,13},{2,10},{6,14},{3,11},{7,15},{16,24},{20,... | collective-permute-start | bytes 294920 | tf_op jit(solution)/shard_map/ppermute | solution.py:337
  39.4 3.5 %copy-start.6 = (bf16[256,256]{1,0:T(8,128)(2,1)}, bf16[256,256]{1,0:T(8,128)(2,1)S(1)}, u32[]{:S(2)}) copy-start(bf16[256,256]{1,0:T(8,128)(2,1)S(1)} %collective-permute-done.3.refs_4_) | copy-start | bytes 393220
  39.4 3.5 %collective-permute-start.8 = (bf16[128,384]{1,0:T(8,128)(2,1)S(1)}, bf16[128,384]{1,0:T(8,128)(2,1)S(1)}, u32[]{:S(2)}, u32[]{:S(2)}) collective-permute-start(bf16[128,384]{1,0:T(8,128)(2,1)S(1)} %add_convert_fusion.1.refs_6_), channel_id=1, source_target_pairs={{0,12},{1,13},{2,14},{3,15},{16,28},{17,29},{18,30},{19,31}} | collective-permute-start | bytes 294920 | tf_op jit(solution)/shard_map/ppermute | solution.py:337
  41.3 1.6 %copy-start.7 = (bf16[256,256]{1,0:T(8,128)(2,1)}, bf16[256,256]{1,0:T(8,128)(2,1)S(1)}, u32[]{:S(2)}) copy-start(bf16[256,256]{1,0:T(8,128)(2,1)S(1)} %collective-permute-done.4.refs_5_) | copy-start | bytes 393220
  41.3 1.6 %copy-start.8 = (bf16[128,384]{1,0:T(8,128)(2,1)}, bf16[128,384]{1,0:T(8,128)(2,1)S(1)}, u32[]{:S(2)}) copy-start(bf16[128,384]{1,0:T(8,128)(2,1)S(1)} %collective-permute-done.6.refs_7_) | copy-start | bytes 294916
  41.6 1.4 %copy-start.9 = (bf16[128,384]{1,0:T(8,128)(2,1)}, bf16[128,384]{1,0:T(8,128)(2,1)S(1)}, u32[]{:S(2)}) copy-start(bf16[128,384]{1,0:T(8,128)(2,1)S(1)} %collective-permute-done.7.refs_8_) | copy-start | bytes 294916
  42.9 0.6 copy-start.10
  43.5 0.7 copy-start.2
  46.9 4.0 %collective-permute-start.9 = (f32[1,6144]{1,0:T(1,128)}, f32[1,6144]{1,0:T(1,128)S(1)}, u32[]{:S(2)}, u32[]{:S(2)}) collective-permute-start(f32[1,6144]{1,0:T(1,128)} %row_stats.1.refs_10_), channel_id=1, source_target_pairs={{0,1},{1,0},{2,3},{3,2},{4,5},{5,4},{6,7},{7,6},{8,9},{9,8},{10,11... | collective-permute-start | bytes 73736 | tf_op jit(solution)/shard_map/ppermute | solution.py:345
  48.4 2.6 %collective-permute-start.10 = (f32[1,6144]{1,0:T(1,128)}, f32[1,6144]{1,0:T(1,128)S(1)}, u32[]{:S(2)}, u32[]{:S(2)}) collective-permute-start(f32[1,6144]{1,0:T(1,128)} %row_stats.1.refs_10_), channel_id=1, source_target_pairs={{0,2},{1,3},{2,0},{3,1},{4,6},{5,7},{6,4},{7,5},{8,10},{9,11},{10,... | collective-permute-start | bytes 73736 | tf_op jit(solution)/shard_map/ppermute | solution.py:345
  48.4 3.5 %collective-permute-start.11 = (f32[1,6144]{1,0:T(1,128)}, f32[1,6144]{1,0:T(1,128)S(1)}, u32[]{:S(2)}, u32[]{:S(2)}) collective-permute-start(f32[1,6144]{1,0:T(1,128)} %row_stats.1.refs_10_), channel_id=1, source_target_pairs={{0,3},{1,2},{2,1},{3,0},{4,7},{5,6},{6,5},{7,4},{8,11},{9,10},{10,... | collective-permute-start | bytes 73736 | tf_op jit(solution)/shard_map/ppermute | solution.py:345
  50.9 0.9 %copy-start.11 = (f32[1,6144]{1,0:T(1,128)}, f32[1,6144]{1,0:T(1,128)S(1)}, u32[]{:S(2)}) copy-start(f32[1,6144]{1,0:T(1,128)S(1)} %collective-permute-done.9.refs_11_) | copy-start | bytes 73732
  50.9 0.9 %copy-start.12 = (f32[1,6144]{1,0:T(1,128)}, f32[1,6144]{1,0:T(1,128)S(1)}, u32[]{:S(2)}) copy-start(f32[1,6144]{1,0:T(1,128)S(1)} %collective-permute-done.10.refs_12_) | copy-start | bytes 73732
  51.8 0.6 copy-start.13
